TPU v7x, 32 devices: a whole 2x2x4 slice. The times are simulated.
32 devices in a mesh: group: 2 (over x), patch: 16 (over z, y, core).
Axes of the slice: x: 2, y: 2, z: 4, core: 2. Of those that a mesh axis runs over, the one named last changes fastest.
Arguments:
- queries: bfloat16 [1024, 1536], P(('group', 'patch')), parts along dimension 0, may hold values from -6 to 6
- keys: bfloat16 [1024, 1536], P(('group', 'patch')), parts along dimension 0, may hold values from -6 to 6
- values: bfloat16 [1024, 1536], P(('group', 'patch')), parts along dimension 0, may hold values from -6 to 6
- stale_keys: bfloat16 [1024, 1536], P(('group', 'patch')), parts along dimension 0, may hold values from -6 to 6
- stale_values: bfloat16 [1024, 1536], P(('group', 'patch')), parts along dimension 0, may hold values from -6 to 6
- text_keys: bfloat16 [32, 512, 1536], P(('group', 'patch')), parts along dimension 0, may hold values from -200 to 200
- text_values: bfloat16 [32, 512, 1536], P(('group', 'patch')), parts along dimension 0, may hold values from -6 to 6
- prompt_device: int32 [2], P('group'), parts along dimension 0, may hold values from 0 to 15
- patch_owner: int32 [32], P('group'), parts along dimension 0, may hold values from 0 to 15, each once
- step: int32 [2], P('group'), parts along dimension 0, may hold values from 0 to 27
- q_gain: float32 [128], replicated, may hold values from 1 to 2.5
- k_gain: float32 [128], replicated, may hold values from 1 to 2.5
- gate_table: float32 [28, 1536], replicated, may hold values from 0.5 to 2
Outputs:
- attended: bfloat16 [1024, 1536], P(('group', 'patch')), parts along dimension 0
There are 2 independent parts, one for each index of `group`. A program takes and returns all parts, laid end to end along the dimension named above; an argument that names none is the same for every part. Nothing has to cross between parts.
Inputs may be any that keep to these rules, and one draw needn't show every extreme that they name: `patch_owner`: A permutation: each patch is held by exactly one device.
All inputs are finite; a program needn't handle non-finite values.
Results may differ from a plain program's by a relative error of at most 0.009.
Values may be sent and summed in bfloat16 or wider, within the bound.
No kernel may reach another device: no remote copies, remote signals or barrier semaphores. Data moves between devices by JAX's collectives and lax.ppermute only.
A program may use at most 128 MiB of HBM per device.

v0:
```python
import jax
import jax.numpy as jnp
from jax import lax
from jax.sharding import PartitionSpec as P

DH = 128
GRID_W = 64
epsilon = 1e-06


def from_partner(shard, axis, bit):
    return lax.ppermute(shard, axis, [(i, i ^ 1 << bit) for i in range(lax.axis_size(axis))])


def broadcast(shard, axis, root):
    mine = lax.axis_index(axis) == root
    return lax.psum(jnp.where(mine, shard, jnp.zeros_like(shard)), axis)


def rms_norm(values_in, gain):
    row_count = values_in.shape[0]
    heads_in = values_in.astype(jnp.float32).reshape(row_count, -1, DH)
    mean_square = jnp.mean(heads_in * heads_in, axis=-1, keepdims=True)
    return heads_in * lax.rsqrt(mean_square + epsilon) * gain


def rope_tables(grid_index):
    grid_row = (grid_index // GRID_W).astype(jnp.float32)
    grid_col = (grid_index % GRID_W).astype(jnp.float32)
    omega = 10000.0 ** (-2.0 * jnp.arange(28, dtype=jnp.float32) / 56.0)
    angle = jnp.concatenate(
        [
            jnp.zeros((grid_index.shape[0], 8), jnp.float32),
            grid_row[:, None] * omega,
            grid_col[:, None] * omega,
        ],
        axis=1,
    )
    return (jnp.cos(angle), jnp.sin(angle))


def rotate(normed, cosine, sine_part):
    row_count, head_count = (normed.shape[0], normed.shape[1])
    paired = normed.reshape(row_count, head_count, DH // 2, 2)
    real_part = paired[..., 0]
    imag_part = paired[..., 1]
    cos_heads = cosine[:, None, :]
    sin_heads = sine_part[:, None, :]
    rotated = jnp.stack(
        [
            cos_heads * real_part - sin_heads * imag_part,
            sin_heads * real_part + cos_heads * imag_part,
        ],
        axis=-1,
    )
    return rotated.reshape(row_count, head_count * DH).astype(jnp.bfloat16)


def partial_softmax(query_local, key_rows, value_rows, key_valid):
    key_count = key_rows.shape[0]
    head_count = query_local.shape[1]
    key_heads = key_rows.reshape(key_count, head_count, DH)
    value_heads = value_rows.reshape(key_count, head_count, DH)
    scores = jnp.einsum(
        "qhd,khd->hqk", query_local, key_heads, preferred_element_type=jnp.float32
    ) * DH ** (-0.5)
    scores = jnp.where(key_valid[None], scores, -1e30)
    highest = jnp.max(scores, axis=-1)
    weights = jnp.where(key_valid[None], jnp.exp(scores - highest[..., None]), 0.0)
    totals = jnp.sum(weights, axis=-1)
    summed = jnp.einsum(
        "hqk,khd->hqd",
        weights.astype(jnp.bfloat16),
        value_heads,
        preferred_element_type=jnp.float32,
    )
    return (highest, totals, summed)


def combine_parts(earlier, later):
    highest = jnp.maximum(earlier[0], later[0])
    factor_early = jnp.exp(earlier[0] - highest)
    factor_late = jnp.exp(later[0] - highest)
    totals = earlier[1] * factor_early + later[1] * factor_late
    summed = earlier[2] * factor_early[..., None] + later[2] * factor_late[..., None]
    return (highest, totals, summed)


def split_swap(piece, bit):
    return from_partner(piece, "patch", bit)


def join_swap(piece, bit):
    return from_partner(piece, "patch", bit)


def order_pair(own_bit, mine, other, axis):
    return jnp.where(own_bit == 0, jnp.stack([mine, other], axis), jnp.stack([other, mine], axis))


def split_heads(stacked, device_index):
    count, tok_rows, feat = stacked.shape
    quarter_width = feat // 4
    low_bit = device_index % 2
    high_bit = device_index // 2 % 2
    shaped = stacked.reshape(count, tok_rows, 2, 2, quarter_width)
    kept = lax.dynamic_index_in_dim(shaped, low_bit, 3, keepdims=False)
    sent = lax.dynamic_index_in_dim(shaped, 1 - low_bit, 3, keepdims=False)
    first = order_pair(low_bit, kept, split_swap(sent, 0), 1)
    kept = lax.dynamic_index_in_dim(first, high_bit, 3, keepdims=False)
    sent = lax.dynamic_index_in_dim(first, 1 - high_bit, 3, keepdims=False)
    second = order_pair(high_bit, kept, split_swap(sent, 1), 1)
    return second.reshape(count, 4 * tok_rows, quarter_width)


def join_heads(block, device_index):
    quad_rows, quarter_width = block.shape
    tok_rows = quad_rows // 4
    low_bit = device_index % 2
    high_bit = device_index // 2 % 2
    shaped = block.reshape(2, 2, tok_rows, quarter_width)
    kept = lax.dynamic_index_in_dim(shaped, high_bit, 0, keepdims=False)
    sent = lax.dynamic_index_in_dim(shaped, 1 - high_bit, 0, keepdims=False)
    first = order_pair(high_bit, kept, join_swap(sent, 1), 0)
    kept = lax.dynamic_index_in_dim(first, low_bit, 1, keepdims=False)
    sent = lax.dynamic_index_in_dim(first, 1 - low_bit, 1, keepdims=False)
    second = order_pair(low_bit, kept, join_swap(sent, 0), 1)
    return second.transpose(2, 0, 1, 3).reshape(tok_rows, 4 * quarter_width)


def gather_quads(pair, device_index):
    levels = lax.axis_size("patch").bit_length() - 1
    current = pair
    for bit in range(2, levels):
        arrived = from_partner(current, "patch", bit)
        own_bit = device_index // (1 << bit) % 2
        current = jnp.where(
            own_bit == 0,
            jnp.concatenate([current, arrived], 1),
            jnp.concatenate([arrived, current], 1),
        )
    return current


def local(
    queries,
    keys,
    values,
    stale_keys,
    stale_values,
    text_keys,
    text_values,
    prompt_device,
    patch_owner,
    step,
    q_gain,
    k_gain,
    gate_table,
):
    tok_rows = queries.shape[0]
    head_count = queries.shape[1] // DH
    device_index = lax.axis_index("patch")
    own_patch = lax.dynamic_index_in_dim(patch_owner, device_index, 0, keepdims=False)
    grid_index = own_patch * tok_rows + jnp.arange(tok_rows, dtype=jnp.int32)
    cosine, sine_part = rope_tables(grid_index)
    query_rot = rotate(rms_norm(queries, q_gain), cosine, sine_part)
    key_rot = rotate(rms_norm(keys, k_gain), cosine, sine_part)
    text_rows, text_vals = (
        broadcast(text_keys[0], "patch", prompt_device[0]),
        broadcast(text_values[0], "patch", prompt_device[0]),
    )
    gate_row = lax.dynamic_index_in_dim(gate_table, step[0], 0, keepdims=False)
    quarter_heads = head_count // 4
    quarter_width = quarter_heads * DH
    quarter = device_index % 4
    spread = split_heads(
        jnp.stack([query_rot, key_rot, values, stale_keys, stale_values]), device_index
    )
    quad_rows = 4 * tok_rows
    query_quad = spread[0].reshape(quad_rows, quarter_heads, DH)
    source = jnp.arange(quad_rows, dtype=jnp.int32) // tok_rows
    own_part = partial_softmax(query_quad, spread[1], spread[2], source[:, None] == source[None, :])
    text_key_quarter = lax.dynamic_slice_in_dim(
        text_rows, quarter * quarter_width, quarter_width, 1
    )
    text_val_quarter = lax.dynamic_slice_in_dim(
        text_vals, quarter * quarter_width, quarter_width, 1
    )
    text_part = partial_softmax(
        query_quad, text_key_quarter, text_val_quarter, jnp.ones((1, text_rows.shape[0]), bool)
    )
    running = combine_parts(own_part, text_part)
    gathered = gather_quads(spread[3:5], device_index)
    key_device = jnp.arange(gathered.shape[1], dtype=jnp.int32) // tok_rows
    query_device = device_index // 4 * 4 + source
    stale_part = partial_softmax(
        query_quad, gathered[0], gathered[1], key_device[None, :] != query_device[:, None]
    )
    highest, totals, summed = combine_parts(running, stale_part)
    mixed = summed / totals[..., None]
    merged = mixed.transpose(1, 0, 2).reshape(quad_rows, quarter_width)
    gate_quarter = lax.dynamic_slice_in_dim(gate_row, quarter * quarter_width, quarter_width, 0)
    return join_heads((merged * gate_quarter).astype(jnp.bfloat16), device_index)


def solution(mesh):
    return jax.shard_map(
        local,
        mesh=mesh,
        in_specs=(
            P(("group", "patch"), None),
            P(("group", "patch"), None),
            P(("group", "patch"), None),
            P(("group", "patch"), None),
            P(("group", "patch"), None),
            P(("group", "patch"), None, None),
            P(("group", "patch"), None, None),
            P("group"),
            P("group"),
            P("group"),
            P(),
            P(),
            P(),
        ),
        out_specs=P(("group", "patch"), None),
        check_vma=False,
    )
```

profile of v0, /device:TPU:0, one launch (start us, length us, event | category | flops | bytes accessed | tf_op | source)
XLA Modules:
  0.0 165.2 jit_solution(5192727807104627779)
XLA Ops:
  6.6 1.1 copy.121
  7.7 0.9 convert_multiply_fusion
  8.6 1.1 copy.119
  9.8 0.6 dynamic_slice.43
  11.1 0.1 reduce_sum.52
  11.3 0.1 reduce_sum.51
  11.6 0.1 mul.263
  11.7 0.1 mul.275
  12.0 0.2 fusion.32
  12.2 0.9 multiply_multiply_fusion
  13.1 2.2 %subtract_convert_fusion = (bf16[32,12,64,1]{0,3,2,1:T(2,128)(2,1)S(1)}, bf16[32,12,64,1]{0,3,2,1:T(2,128)(2,1)S(1)}, bf16[32,12,64,1]{0,3,2,1:T(2,128)(2,1)S(1)}, bf16[32,12,64,1]{0,3,2,1:T(2,128)(2,1)S(1)}) fusion(f32[32,12,64,2]{0,3,2,1:T(2,128)S(1)} %get-tuple-element.45, f32[32,64]{0,1:T(8,128)S(1)} %get-tuple-element.32, ...), kind=kLoop, calls=%fused_computation.35 | loop fusion | flops 393216 | bytes 606208 | tf_op jit(solution)/shard_map/convert
  15.3 1.0 pad_maximum_fusion.1
  16.4 0.2 copy.124
  16.5 1.0 pad_maximum_fusion
  17.6 0.2 copy.123
  18.0 0.9 dynamic-slice_bitcast_fusion.3
  18.9 0.5 collective-permute-start
  20.1 0.7 copy.132
  20.8 1.7 %copy.135 = bf16[1,512,1536]{1,2,0:T(8,128)(2,1)S(1)} copy(bf16[1,512,1536]{2,1,0:T(8,128)(2,1)} %param.19) | data formatting | bytes 3145728 | tf_op args[6]
  22.5 1.9 %select_bitcast_fusion = (bf16[512,1536]{0,1:T(8,128)(2,1)}, bf16[512,1536]{0,1:T(8,128)(2,1)}) fusion(bf16[1,512,1536]{1,2,0:T(8,128)(2,1)S(1)} %copy.135, pred[]{:T(512)S(6)} %eq.56, bf16[1,512,1536]{1,2,0:T(8,128)(2,1)S(1)} %copy.132), kind=kLoop, calls=%fused_computation | loop fusion | flops 1572864 | bytes 6291457 | tf_op jit(solution)/shard_map/jit(_where)/select_n | solution.py:17
  24.5 0.8 copy-done.2
  25.4 1.1 maximum_select_fusion.1
  26.6 2.6 %collective-permute-start.1 = (bf16[5,2,32,384]{3,2,1,0:T(8,128)(2,1)S(1)}, bf16[5,2,32,384]{3,2,1,0:T(8,128)(2,1)S(1)}, u32[]{:S(2)}, u32[]{:S(2)}) collective-permute-start(bf16[5,2,32,384]{3,2,1,0:T(8,128)(2,1)S(1)} %get-tuple-element.22), channel_id=1, source_target_pairs={{0,2},{1,3},{2,0},{3,1},{4,6},{5,7},{6,4},{7,5},{8,10},{9,11},{10,... | collective-permute-start | bytes 737288 | tf_op jit(solution)/shard_map/ppermute | solution.py:12
  29.3 9.0 %collective-permute-done.1 = bf16[5,2,32,384]{3,2,1,0:T(8,128)(2,1)S(1)} collective-permute-done((bf16[5,2,32,384]{3,2,1,0:T(8,128)(2,1)S(1)}, bf16[5,2,32,384]{3,2,1,0:T(8,128)(2,1)S(1)}, u32[]{:S(2)}, u32[]{:S(2)}) %collective-permute-start.1) | collective-permute-done | bytes 245792 | tf_op jit(solution)/shard_map/ppermute | solution.py:12
  38.4 1.5 collective-permute-start.2
  40.8 8.6 %collective-permute-done.2 = bf16[2,128,384]{2,1,0:T(8,128)(2,1)S(1)} collective-permute-done((bf16[2,128,384]{2,1,0:T(8,128)(2,1)S(1)}, bf16[2,128,384]{2,1,0:T(8,128)(2,1)S(1)}, u32[]{:S(2)}, u32[]{:S(2)}) %collective-permute-start.2) | collective-permute-done | bytes 196640 | tf_op jit(solution)/shard_map/ppermute | solution.py:12
  49.4 0.1 maximum_select_fusion.3
  49.6 2.7 %collective-permute-start.3 = (bf16[2,256,384]{2,1,0:T(8,128)(2,1)S(1)}, bf16[2,256,384]{2,1,0:T(8,128)(2,1)S(1)}, u32[]{:S(2)}, u32[]{:S(2)}) collective-permute-start(bf16[2,256,384]{2,1,0:T(8,128)(2,1)S(1)} %maximum_select_fusion.3), channel_id=1, source_target_pairs={{0,8},{1,9},{2,10},{3,11},{4,12},{5,13},{6,14},{7,15},{8,0},{9,1},... | collective-permute-start | bytes 1179656 | tf_op jit(solution)/shard_map/ppermute | solution.py:12
  52.4 0.2 fusion.55
  52.7 24.7 %collective-permute-done.3 = bf16[2,256,384]{2,1,0:T(8,128)(2,1)S(1)} collective-permute-done((bf16[2,256,384]{2,1,0:T(8,128)(2,1)S(1)}, bf16[2,256,384]{2,1,0:T(8,128)(2,1)S(1)}, u32[]{:S(2)}, u32[]{:S(2)}) %collective-permute-start.3) | collective-permute-done | bytes 393248 | tf_op jit(solution)/shard_map/ppermute | solution.py:12
  77.3 0.3 maximum_select_fusion
  77.7 0.2 copy.138
  77.9 0.2 copy.141
  78.1 0.3 fusion.53
  78.5 0.3 fusion.11
  78.8 69.3 %all-reduce.3.cloned.1.call-done = (bf16[512,1536]{0,1:T(8,128)(2,1)}, bf16[512,1536]{0,1:T(8,128)(2,1)}) async-done(((bf16[512,1536]{0,1:T(8,128)(2,1)}, bf16[512,1536]{0,1:T(8,128)(2,1)}), (bf16[512,1536]{0,1:T(8,128)(2,1)}, bf16[512,1536]{0,1:T(8,128)(2,1)})) %all-reduce.3.cloned.1.call-update) | async-done | bytes 3145744 | tf_op jit(solution)/shard_map/psum | solution.py:17
  148.1 1.0 constant_dynamic-slice_fusion.3
  149.1 0.3 fusion.54
  149.4 1.0 constant_dynamic-slice_fusion.2
  150.5 0.3 fusion.9
  150.8 0.2 fusion.6
  151.0 0.3 fusion.8
  151.4 0.4 fusion.7
  151.7 0.1 copy.143
  152.1 1.0 collective-permute-start.4
  153.1 3.1 %collective-permute-done.4 = bf16[2,32,384]{2,1,0:T(8,128)(2,1)S(1)} collective-permute-done((bf16[2,32,384]{2,1,0:T(8,128)(2,1)S(1)}, bf16[2,32,384]{2,1,0:T(8,128)(2,1)S(1)}, u32[]{:S(2)}, u32[]{:S(2)}) %collective-permute-start.4) | collective-permute-done | bytes 49184 | tf_op jit(solution)/shard_map/ppermute | solution.py:12
  156.3 1.2 collective-permute-done.5
  157.7 0.7 reshape.361
  (66 shorter events, 1.8 us)
Async XLA Ops:
  6.5 34.2 %copy-start = (f32[28,1536]{1,0:T(8,128)S(1)}, f32[28,1536]{1,0:T(8,128)}, u32[]{:S(2)}) copy-start(f32[28,1536]{1,0:T(8,128)} %param.25) | copy-start | bytes 516100
  6.5 3.2 %copy-start.3 = (bf16[32,1536]{1,0:T(8,128)(2,1)S(1)}, bf16[32,1536]{1,0:T(8,128)(2,1)}, u32[]{:S(2)}) copy-start(bf16[32,1536]{1,0:T(8,128)(2,1)} %param.13) | copy-start | bytes 294916
  6.5 3.2 %copy-start.9 = (s32[16]{0:T(128)S(1)}, s32[16]{0:T(128)}, u32[]{:S(2)}) copy-start(s32[16]{0:T(128)} %param.21) | copy-start | bytes 196
  6.5 141.5 %all-reduce.3.cloned.1.call-start = ((), (), s32[]{:S(2)}) async-start(), calls=%async_computation | async-start | bytes 6291456 | tf_op jit(solution)/shard_map/psum | solution.py:17
  7.7 3.9 %copy-start.7 = (f32[128]{0:T(128)S(1)}, f32[128]{0:T(128)}, u32[]{:S(2)}) copy-start(f32[128]{0:T(128)} %param.23) | copy-start | bytes 1540
  7.7 4.0 %copy-start.8 = (f32[128]{0:T(128)S(1)}, f32[128]{0:T(128)}, u32[]{:S(2)}) copy-start(f32[128]{0:T(128)} %param.24) | copy-start | bytes 1540
  15.3 2.5 %copy-start.4 = (bf16[32,1536]{1,0:T(8,128)(2,1)S(1)}, bf16[32,1536]{1,0:T(8,128)(2,1)}, u32[]{:S(2)}) copy-start(bf16[32,1536]{1,0:T(8,128)(2,1)} %param.15) | copy-start | bytes 294916
  16.3 1.5 copy-start.5
  16.3 1.5 copy-start.6
  17.6 2.5 %copy-start.1 = (bf16[1,512,1536]{2,1,0:T(8,128)(2,1)S(1)}, bf16[1,512,1536]{2,1,0:T(8,128)(2,1)}, u32[]{:S(2)}) copy-start(bf16[1,512,1536]{2,1,0:T(8,128)(2,1)} %param.18) | copy-start | bytes 4718596
  18.9 5.6 %collective-permute-start = (bf16[5,32,2,384]{3,1,2,0:T(8,128)(2,1)}, bf16[5,32,2,384]{3,1,2,0:T(8,128)(2,1)}, u32[]{:S(2)}, u32[]{:S(2)}) collective-permute-start(bf16[5,32,2,384]{3,1,2,0:T(8,128)(2,1)} %get-tuple-element.24), channel_id=1, source_target_pairs={{0,1},{1,0},{2,3},{3,2},{4,5},{5,4},{6,7},{7,6},{8,9},{9,8},{10,11... | collective-permute-start | bytes 737288 | tf_op jit(solution)/shard_map/ppermute | solution.py:12
  24.4 0.9 copy-start.2
  26.6 11.7 %collective-permute-start.1 = (bf16[5,2,32,384]{3,2,1,0:T(8,128)(2,1)S(1)}, bf16[5,2,32,384]{3,2,1,0:T(8,128)(2,1)S(1)}, u32[]{:S(2)}, u32[]{:S(2)}) collective-permute-start(bf16[5,2,32,384]{3,2,1,0:T(8,128)(2,1)S(1)} %get-tuple-element.22), channel_id=1, source_target_pairs={{0,2},{1,3},{2,0},{3,1},{4,6},{5,7},{6,4},{7,5},{8,10},{9,11},{10,... | collective-permute-start | bytes 737288 | tf_op jit(solution)/shard_map/ppermute | solution.py:12
  38.4 11.0 %collective-permute-start.2 = (bf16[2,128,384]{2,1,0:T(8,128)(2,1)S(1)}, bf16[2,128,384]{2,1,0:T(8,128)(2,1)S(1)}, u32[]{:S(2)}, u32[]{:S(2)}) collective-permute-start(bf16[2,128,384]{2,1,0:T(8,128)(2,1)S(1)} %bitcast.139), channel_id=1, source_target_pairs={{0,4},{1,5},{2,6},{3,7},{4,0},{5,1},{6,2},{7,3},{8,12},{9,13},{10,... | collective-permute-start | bytes 589832 | tf_op jit(solution)/shard_map/ppermute | solution.py:12
  49.6 27.8 %collective-permute-start.3 = (bf16[2,256,384]{2,1,0:T(8,128)(2,1)S(1)}, bf16[2,256,384]{2,1,0:T(8,128)(2,1)S(1)}, u32[]{:S(2)}, u32[]{:S(2)}) collective-permute-start(bf16[2,256,384]{2,1,0:T(8,128)(2,1)S(1)} %maximum_select_fusion.3), channel_id=1, source_target_pairs={{0,8},{1,9},{2,10},{3,11},{4,12},{5,13},{6,14},{7,15},{8,0},{9,1},... | collective-permute-start | bytes 1179656 | tf_op jit(solution)/shard_map/ppermute | solution.py:12
  152.1 4.2 %collective-permute-start.4 = (bf16[2,32,384]{2,1,0:T(8,128)(2,1)S(1)}, bf16[2,32,384]{2,1,0:T(8,128)(2,1)S(1)}, u32[]{:S(2)}, u32[]{:S(2)}) collective-permute-start(bf16[2,32,384]{2,1,0:T(8,128)(2,1)S(1)} %get-tuple-element.28), channel_id=1, source_target_pairs={{0,2},{1,3},{2,0},{3,1},{4,6},{5,7},{6,4},{7,5},{8,10},{9,11},{10,... | collective-permute-start | bytes 147464 | tf_op jit(solution)/shard_map/ppermute | solution.py:12
  156.3 1.3 collective-permute-start.5
Sparse Core Ops, SparseCore 0:
  24.6 123.4 all-reduce.2
where the time goes:
time: 166 us; the launch traced here: 165 us
  waiting for transfers between devices  116 us (70%)
  between operations  16 us (10%)
  local copies, waits for them, and re-layouts  11.9 us (7%)
  other arithmetic  11.2 us (7%)
  starting transfers between devices  8.3 us (5%)
  matrix products  1.84 us (1%)
    psum x1, waiting for transfers between devices, broadcast(): return lax.psum(jnp.where(mine, shard, jnp.zeros_like(shard)), axis)  69.3 us
    ppermute x6, waiting for transfers between devices, from_partner(): lax.ppermute(shard, axis, [(i, i ^ 1 << bit) for i in range(lax.axis_size...  46.6 us
    ppermute x6, starting transfers between devices, from_partner(): lax.ppermute(shard, axis, [(i, i ^ 1 << bit) for i in range(lax.axis_size...  8.3 us
    unnamed x26, local copies, waits for them, and re-layouts  3.39 us
  transfers between devices with their start and end apart: 7, of which 6 were waited for; matrix products, arithmetic and copies ran while one was open for 5% of the time, Pallas kernels for 0%

commit v1 on v0

--- a/solution.py
+++ b/solution.py
@@ -14,7 +14,7 @@
 
 def broadcast(shard, axis, root):
     mine = lax.axis_index(axis) == root
-    return lax.psum(jnp.where(mine, shard, jnp.zeros_like(shard)), axis)
+    return jnp.sum(lax.all_gather(jnp.where(mine, shard, jnp.zeros_like(shard)), axis), axis=0)
 
 
 def rms_norm(values_in, gain):

time: 166 us -> 319 us (1.92)
  waiting for transfers between devices: 116 us -> 243 us
  other arithmetic: 11.2 us -> 38.3 us
    all_gather x0 -> x2, waiting for transfers between devices: none -> 190 us  [broadcast(): lax.all_gather(jnp.where(mine, shard, jnp.zeros_like(shard)), axis)]
    psum x1 -> x0, waiting for transfers between devices: 69.3 us -> none  [broadcast(): return lax.psum(jnp.where(mine, shard, jnp.zeros_like(shard)), axis)]
    reduce_sum x0 -> x2, other arithmetic: none -> 28.7 us  [broadcast(): jnp.sum(lax.all_gather(jnp.where(mine, shard, jnp.zeros_like(shard)), axi...]
    ppermute x6, waiting for transfers between devices: 46.6 us -> 52.5 us  [from_partner(): lax.ppermute(shard, axis, [(i, i ^ 1 << bit) for i in range(lax.axis_size...]
  transfers between devices with their start and end apart: 7 -> 8, of which waited for: 6 -> 8; matrix products, arithmetic and copies ran while one was open for 5% -> 9% of each run, Pallas kernels for 0% -> 0%
where the time goes in v1:
time: 319 us; the launch traced here: 318 us
  waiting for transfers between devices  243 us (76%)
  other arithmetic  38.3 us (12%)
  between operations  16 us (5%)
  local copies, waits for them, and re-layouts  9.63 us (3%)
  starting transfers between devices  8.61 us (3%)
    all_gather x2, waiting for transfers between devices, broadcast(): lax.all_gather(jnp.where(mine, shard, jnp.zeros_like(shard)), axis)  190 us
    ppermute x6, waiting for transfers between devices, from_partner(): lax.ppermute(shard, axis, [(i, i ^ 1 << bit) for i in range(lax.axis_size...  52.5 us
    reduce_sum x2, other arithmetic, broadcast(): jnp.sum(lax.all_gather(jnp.where(mine, shard, jnp.zeros_like(shard)), axi...  28.7 us
    ppermute x6, starting transfers between devices, from_partner(): lax.ppermute(shard, axis, [(i, i ^ 1 << bit) for i in range(lax.axis_size...  8.57 us
  transfers between devices with their start and end apart: 8, of which 8 were waited for; matrix products, arithmetic and copies ran while one was open for 9% of the time, Pallas kernels for 0%

profile of v1, /device:TPU:0, one launch (start us, length us, event | category | flops | bytes accessed | tf_op | source)
XLA Modules:
  0.0 318.1 jit_solution(12642668951874692974)
XLA Ops:
  7.2 1.2 broadcast_select_fusion.1
  8.5 1.3 copy-done.2
  9.9 1.2 broadcast_select_fusion
  11.2 0.8 copy-done.8
  12.0 0.2 copy.115
  12.2 0.2 copy.117
  12.5 0.1 reduce_sum.76
  13.0 0.1 mul.263
  13.3 0.6 dynamic_slice.43
  14.7 0.2 fusion.32
  14.9 0.9 multiply_multiply_fusion
  15.8 2.1 subtract_convert_fusion
  17.9 1.0 pad_maximum_fusion.1
  19.0 0.2 copy.120
  19.2 1.0 pad_maximum_fusion
  20.2 0.2 copy.119
  20.7 0.6 collective-permute-start
  21.3 1.1 collective-permute-done
  22.6 2.9 collective-permute-start.1
  26.2 0.7 dynamic-slice_reduce_fusion
  27.0 10.4 %collective-permute-done.1 = bf16[5,2,32,384]{3,2,1,0:T(8,128)(2,1)S(1)} collective-permute-done((bf16[5,2,32,384]{3,2,1,0:T(8,128)(2,1)S(1)}, bf16[5,2,32,384]{3,2,1,0:T(8,128)(2,1)S(1)}, u32[]{:S(2)}, u32[]{:S(2)}) %collective-permute-start.1) | collective-permute-done | bytes 245792 | tf_op jit(solution)/shard_map/ppermute | solution.py:12
  37.8 11.5 %collective-permute-done.2 = bf16[2,128,384]{2,1,0:T(8,128)(2,1)S(1)} collective-permute-done((bf16[2,128,384]{2,1,0:T(8,128)(2,1)S(1)}, bf16[2,128,384]{2,1,0:T(8,128)(2,1)S(1)}, u32[]{:S(2)}, u32[]{:S(2)}) %collective-permute-start.2) | collective-permute-done | bytes 196640 | tf_op jit(solution)/shard_map/ppermute | solution.py:12
  49.4 3.6 %collective-permute-start.3 = (bf16[2,256,384]{2,1,0:T(8,128)(2,1)S(1)}, bf16[2,256,384]{2,1,0:T(8,128)(2,1)S(1)}, u32[]{:S(2)}, u32[]{:S(2)}) collective-permute-start(bf16[2,256,384]{2,1,0:T(8,128)(2,1)S(1)} %maximum_select_fusion.3), channel_id=1, source_target_pairs={{0,8},{1,9},{2,10},{3,11},{4,12},{5,13},{6,14},{7,15},{8,0},{9,1},... | collective-permute-start | bytes 1179656 | tf_op jit(solution)/shard_map/ppermute | solution.py:12
  53.2 0.7 reshape_squeeze.17
  53.9 0.2 fusion.55
  54.2 25.3 %collective-permute-done.3 = bf16[2,256,384]{2,1,0:T(8,128)(2,1)S(1)} collective-permute-done((bf16[2,256,384]{2,1,0:T(8,128)(2,1)S(1)}, bf16[2,256,384]{2,1,0:T(8,128)(2,1)S(1)}, u32[]{:S(2)}, u32[]{:S(2)}) %collective-permute-start.3) | collective-permute-done | bytes 393248 | tf_op jit(solution)/shard_map/ppermute | solution.py:12
  79.5 0.3 maximum_select_fusion
  79.9 0.2 copy.134
  80.1 0.9 copy.137
  81.0 0.3 fusion.53
  81.4 0.3 fusion.11
  81.7 71.2 %all-gather.3.cloned.1.call-done = bf16[16,512,1536]{2,1,0:T(8,128)(2,1)} async-done(((bf16[1,512,1536]{2,1,0:T(8,128)(2,1)}), bf16[16,512,1536]{2,1,0:T(8,128)(2,1)}) %all-gather.3.cloned.1.call-update) | async-done | bytes 25165840 | tf_op jit(solution)/shard_map/all_gather | solution.py:17
  152.9 14.1 %reduce_sum.77 = bf16[512,1536]{1,0:T(8,128)(2,1)S(1)} reduce(bf16[16,512,1536]{2,1,0:T(8,128)(2,1)} %all-gather.3.cloned.1.call-done, bf16[]{:T(256)} %constant.208.clone.1), dimensions={0}, to_apply=%region_3.4 | reduce | flops 11796480 | bytes 26738690 | tf_op jit(solution)/shard_map/reduce_sum | solution.py:17
  166.9 119.3 %all-gather.5.cloned.1.call-done = bf16[16,512,1536]{2,1,0:T(8,128)(2,1)} async-done(((bf16[1,512,1536]{2,1,0:T(8,128)(2,1)}), bf16[16,512,1536]{2,1,0:T(8,128)(2,1)}) %all-gather.5.cloned.1.call-update) | async-done | bytes 25165840 | tf_op jit(solution)/shard_map/all_gather | solution.py:17
  286.3 14.6 %reduce_sum.78 = bf16[512,1536]{1,0:T(8,128)(2,1)} reduce(bf16[16,512,1536]{2,1,0:T(8,128)(2,1)} %all-gather.5.cloned.1.call-done, bf16[]{:T(256)} %constant.208.clone.1), dimensions={0}, to_apply=%region_5.6 | reduce | flops 11796480 | bytes 26738690 | tf_op jit(solution)/shard_map/reduce_sum | solution.py:17
  300.8 1.1 constant_dynamic-slice_fusion.2
  301.9 0.2 copy.128
  302.1 0.3 fusion.54
  302.5 0.2 copy.131
  302.7 0.3 fusion.9
  303.0 0.8 fusion.6
  303.9 0.3 fusion.8
  304.3 0.4 fusion.7
  304.6 0.1 copy.139
  305.0 1.3 collective-permute-start.4
  306.2 2.9 collective-permute-done.4
  309.2 1.2 collective-permute-done.5
  310.6 0.7 reshape.355
  (89 shorter events, 2.4 us)
Async XLA Ops:
  6.5 19.7 %copy-start = (f32[28,1536]{1,0:T(8,128)S(1)}, f32[28,1536]{1,0:T(8,128)}, u32[]{:S(2)}) copy-start(f32[28,1536]{1,0:T(8,128)} %param.25) | copy-start | bytes 516100
  6.5 146.3 %all-gather.3.cloned.1.call-start = ((), (), s32[]{:S(2)}) async-start(), calls=%async_computation | async-start | bytes 26738688 | tf_op jit(solution)/shard_map/all_gather | solution.py:17
  8.5 1.4 copy-start.2
  8.5 277.8 %all-gather.5.cloned.1.call-start = ((), (), s32[]{:S(2)}) async-start(), calls=%async_computation.1 | async-start | bytes 26738688 | tf_op jit(solution)/shard_map/all_gather | solution.py:17
  11.1 0.9 copy-start.8
  11.1 1.1 copy-start.7
  12.2 0.8 copy-start.16
  12.2 0.9 copy-start.17
  12.2 1.1 copy-start.18
  17.9 2.5 copy-start.9
  17.9 2.5 copy-start.10
  19.0 1.5 copy-start.11
  20.7 1.7 collective-permute-start
  22.6 14.9 %collective-permute-start.1 = (bf16[5,2,32,384]{3,2,1,0:T(8,128)(2,1)S(1)}, bf16[5,2,32,384]{3,2,1,0:T(8,128)(2,1)S(1)}, u32[]{:S(2)}, u32[]{:S(2)}) collective-permute-start(bf16[5,2,32,384]{3,2,1,0:T(8,128)(2,1)S(1)} %get-tuple-element.20), channel_id=1, source_target_pairs={{0,2},{1,3},{2,0},{3,1},{4,6},{5,7},{6,4},{7,5},{8,10},{9,11},{10,... | collective-permute-start | bytes 737288 | tf_op jit(solution)/shard_map/ppermute | solution.py:12
  27.0 54.4 %copy-start.3 = (pred[128,512]{1,0:T(8,128)(4,1)}, pred[128,512]{1,0:T(8,128)(4,1)S(1)}, u32[]{:S(2)}) copy-start(pred[128,512]{1,0:T(8,128)(4,1)S(1)} %broadcast_compare_fusion) | copy-start | bytes 196612
  37.6 11.7 %collective-permute-start.2 = (bf16[2,128,384]{2,1,0:T(8,128)(2,1)S(1)}, bf16[2,128,384]{2,1,0:T(8,128)(2,1)S(1)}, u32[]{:S(2)}, u32[]{:S(2)}) collective-permute-start(bf16[2,128,384]{2,1,0:T(8,128)(2,1)S(1)} %bitcast.135), channel_id=1, source_target_pairs={{0,4},{1,5},{2,6},{3,7},{4,0},{5,1},{6,2},{7,3},{8,12},{9,13},{10,... | collective-permute-start | bytes 589832 | tf_op jit(solution)/shard_map/ppermute | solution.py:12
  49.4 30.1 %collective-permute-start.3 = (bf16[2,256,384]{2,1,0:T(8,128)(2,1)S(1)}, bf16[2,256,384]{2,1,0:T(8,128)(2,1)S(1)}, u32[]{:S(2)}, u32[]{:S(2)}) collective-permute-start(bf16[2,256,384]{2,1,0:T(8,128)(2,1)S(1)} %maximum_select_fusion.3), channel_id=1, source_target_pairs={{0,8},{1,9},{2,10},{3,11},{4,12},{5,13},{6,14},{7,15},{8,0},{9,1},... | collective-permute-start | bytes 1179656 | tf_op jit(solution)/shard_map/ppermute | solution.py:12
  54.1 248.9 %copy-start.12 = (f32[3,128]{1,0:T(4,128)}, f32[3,128]{1,0:T(4,128)S(1)}, u32[]{:S(2)}) copy-start(f32[3,128]{1,0:T(4,128)S(1)} %get-tuple-element.37) | copy-start | bytes 4612
  81.4 221.6 %copy-start.13 = (f32[3,128]{1,0:T(4,128)}, f32[3,128]{1,0:T(4,128)S(1)}, u32[]{:S(2)}) copy-start(f32[3,128]{1,0:T(4,128)S(1)} %get-tuple-element.33) | copy-start | bytes 4612
  302.1 0.9 copy-start.5
  302.6 1.6 copy-start.4
  302.7 1.6 copy-start.6
  303.0 1.3 copy-start.14
  304.2 0.7 copy-start.15
  304.3 7.0 %copy-start.1 = (f32[28,1536]{1,0:T(8,128)S(1)}, f32[28,1536]{1,0:T(8,128)}, u32[]{:S(2)}) copy-start(f32[28,1536]{1,0:T(8,128)} %param.25) | copy-start | bytes 516100
  305.0 4.2 %collective-permute-start.4 = (bf16[2,32,384]{2,1,0:T(8,128)(2,1)S(1)}, bf16[2,32,384]{2,1,0:T(8,128)(2,1)S(1)}, u32[]{:S(2)}, u32[]{:S(2)}) collective-permute-start(bf16[2,32,384]{2,1,0:T(8,128)(2,1)S(1)} %get-tuple-element.26), channel_id=1, source_target_pairs={{0,2},{1,3},{2,0},{3,1},{4,6},{5,7},{6,4},{7,5},{8,10},{9,11},{10,... | collective-permute-start | bytes 147464 | tf_op jit(solution)/shard_map/ppermute | solution.py:12
  309.2 1.3 collective-permute-start.5
Sparse Core Ops, SparseCore 0:
  8.9 143.8 all-gather.2
  154.4 131.7 all-gather.4
